TPU v7x, 128 devices: a whole 4x4x4 slice. The times are simulated.
128 devices in a mesh: seq: 8 (over z, core), tp: 16 (over x, y).
Axes of the slice: x: 4, y: 4, z: 4, core: 2. Of those that a mesh axis runs over, the one named last changes fastest.
Arguments:
- patches: bfloat16 [32768, 1280], P(('seq', 'tp')), may hold values from -6 to 6
- image_table: int32 [256, 3], replicated, may hold values from 0 to 4095, as said below
- ln_gain: float32 [1280], replicated, may hold values from 0.25 to 1.75
- ln_bias: float32 [1280], replicated, may hold values from -3 to 3
- merge_up: bfloat16 [5120, 5120], P(None, 'tp'), may hold values from -0.078125 to 0.078125
- merge_up_bias: float32 [5120], P('tp'), may hold values from -3 to 3
- merge_down: bfloat16 [5120, 3584], P('tp'), may hold values from -0.15625 to 0.15625
- merge_down_bias: float32 [3584], replicated, may hold values from -3 to 3
- text_embeds: bfloat16 [4096, 3584], P('seq', 'tp'), may hold values from -6 to 6
- attn_gain: float32 [3584], replicated, may hold values from 0.25 to 1.75
- q_weight: bfloat16 [3584, 2048], P(None, 'tp'), may hold values from -2 to 2
- q_bias: float32 [2048], P('tp'), may hold values from -3 to 3
- key_value_weight: bfloat16 [3584, 1024], replicated, may hold values from -2 to 2
- key_value_bias: float32 [1024], replicated, may hold values from -3 to 3
- o_weight: bfloat16 [2048, 3584], P('tp'), may hold values from -0.1875 to 0.1875
Outputs:
- block_out: bfloat16 [4096, 3584], P('seq', 'tp')
Inputs may be any that keep to these rules, and one draw needn't show every extreme that they name: `image_table`: grid entries are even. Table rows 2d and 2d + 1 are the two images of device d = seq index * 16 + tp index; the second starts right after the first, so the device's tokens fill consecutive positions inside block [s * 512, (s + 1) * 512) of its seq index s. Images never intersect. The two images of a device hold at most 64 merged tokens, and in every seq group one device holds exactly 64. A sequence block holds at most 424 image tokens, and some block holds exactly that many.
All inputs are finite; a program needn't handle non-finite values.
Results may differ from a plain program's by a relative error of at most 0.012.
Values may be sent and summed in bfloat16 or wider, within the bound.
A program may use at most 128 MiB of HBM per device.

v0:
```python
import jax
import jax.numpy as jnp
from jax import lax
from jax.sharding import PartitionSpec as P

HEAD_DIMENSION = 128
KEY_VALUE_HEADS = 4
LOCAL_QUERY_HEAD = 16
CAP = 64
TOK_SEQ = 512
MW = 5120
EPS = 1e-06
THETA = 1000000.0


def sent_together(arrays, axis, dim, along):
    both = jnp.concatenate(arrays, axis=along)
    out, at, done = (lax.all_gather(both, axis, axis=dim, tiled=True), 0, [])
    for a in arrays:
        done.append(lax.slice_in_dim(out, at, at + a.shape[along], axis=along))
        at += a.shape[along]
    return tuple(done)


def copy_for_each(shard, axis):
    peers = lax.axis_size(axis)
    return lax.all_to_all(
        jnp.broadcast_to(shard[None], (peers, *shard.shape)), axis, 0, 0, tiled=True
    )


def laid_out(pieces, dim):
    lengths = list(pieces.shape[1:])
    lengths[dim] *= pieces.shape[0]
    return jnp.moveaxis(pieces, 0, dim).reshape(lengths)


def gathered_copies(shard, axis, dim):
    pieces = copy_for_each(shard, axis)
    return laid_out(pieces, dim)


def layer_norm(row_data, scale_row, offset_row):
    centre = jnp.mean(row_data, axis=-1, keepdims=True)
    centred = row_data - centre
    spread = jnp.mean(centred * centred, axis=-1, keepdims=True)
    return centred * lax.rsqrt(spread + EPS) * scale_row + offset_row


def image_fields(image_table):
    grid_h = image_table[:, 0]
    grid_w = image_table[:, 1]
    across = grid_w // 2
    return (across, grid_h // 2 * across, image_table[:, 2])


def rope_tables(positions, image_table, head_size):
    across, counts, offsets = image_fields(image_table)
    inside = (
        (positions[:, None] >= offsets[None, :])
        & (positions[:, None] < (offsets + counts)[None, :])
    ).astype(jnp.int32)
    is_image = jnp.sum(inside, axis=1)
    run_start = jnp.sum(inside * offsets[None, :], axis=1)
    row_width = jnp.sum(inside * across[None, :], axis=1) + (1 - is_image)
    inner_index = positions - run_start
    pos_t = jnp.where(is_image > 0, run_start, positions)
    pos_h = jnp.where(is_image > 0, run_start + inner_index // row_width, positions)
    pos_w = jnp.where(is_image > 0, run_start + inner_index % row_width, positions)
    half_size = head_size // 2
    frequency = jnp.arange(half_size, dtype=jnp.int32)
    inverse = THETA ** (-2.0 * frequency.astype(jnp.float32) / head_size)
    first_cut = head_size // 8
    second_cut = first_cut + 3 * head_size // 16
    chosen = jnp.where(
        frequency[None, :] < first_cut,
        pos_t[:, None],
        jnp.where(frequency[None, :] < second_cut, pos_h[:, None], pos_w[:, None]),
    )
    angles = chosen.astype(jnp.float32) * inverse[None, :]
    angles = jnp.concatenate([angles, angles], axis=1)
    return (jnp.cos(angles), jnp.sin(angles), is_image)


def apply_rotation(value_tensor, cosine_values, sine_lookup):
    half_size = value_tensor.shape[-1] // 2
    turned = jnp.concatenate(
        [-value_tensor[..., half_size:], value_tensor[..., :half_size]], axis=-1
    )
    return value_tensor * cosine_values[:, None, :] + turned * sine_lookup[:, None, :]


def merger_hidden(vision, merge_up, merge_up_bias, image_weight):
    lifted = jnp.dot(vision, merge_up, preferred_element_type=jnp.float32) + merge_up_bias
    return (jax.nn.gelu(lifted, approximate=False) * image_weight[:, None]).astype(jnp.bfloat16)


def per_device(
    patches,
    image_table,
    ln_gain,
    ln_bias,
    merge_up,
    merge_up_bias,
    merge_down,
    merge_down_bias,
    text_embeds,
    attn_gain,
    q_weight,
    q_bias,
    key_value_weight,
    key_value_bias,
    o_weight,
):
    tp_count = lax.axis_size("tp")
    seq_index = lax.axis_index("seq")
    tensor_parallel_index = lax.axis_index("tp")
    row_share = TOK_SEQ // tp_count
    column_count = text_embeds.shape[1]
    local_heads = q_weight.shape[1] // HEAD_DIMENSION
    normed = layer_norm(patches.astype(jnp.float32), ln_gain, ln_bias).astype(jnp.bfloat16)
    merged = normed.reshape(CAP, MW)
    block_index = jnp.arange(TOK_SEQ, dtype=jnp.int32)
    positions = seq_index * TOK_SEQ + block_index % row_share * tp_count + block_index // row_share
    cosine_values, sine_lookup, is_image = rope_tables(positions, image_table, HEAD_DIMENSION)
    image_weight = is_image.astype(jnp.float32)
    across, counts, offsets = image_fields(image_table)
    group_begin = 2 * seq_index * tp_count
    group_first = lax.dynamic_slice_in_dim(offsets, group_begin, 2 * tp_count).reshape(tp_count, 2)[
        :, 0
    ]
    group_length = jnp.sum(
        lax.dynamic_slice_in_dim(counts, group_begin, 2 * tp_count).reshape(tp_count, 2), axis=1
    )
    run_start = group_first[tensor_parallel_index]
    run_length = group_length[tensor_parallel_index]
    per_peer = CAP // tp_count + 1
    residue = run_start % tp_count
    slot_index = (
        jnp.arange(tp_count, dtype=jnp.int32)[:, None]
        + jnp.arange(per_peer, dtype=jnp.int32)[None, :] * tp_count
        - residue
    ).reshape(-1)
    live_slot = (slot_index >= 0) & (slot_index < run_length)
    picker = (
        (slot_index[:, None] == jnp.arange(CAP, dtype=jnp.int32)[None, :]) & live_slot[:, None]
    ).astype(jnp.bfloat16)
    outgoing = (
        jnp.dot(picker, merged, preferred_element_type=jnp.float32)
        .astype(jnp.bfloat16)
        .reshape(tp_count, per_peer, MW)
    )
    incoming = lax.all_to_all(outgoing, "tp", split_axis=0, concat_axis=0, tiled=True)
    target = (
        group_first[:, None] // tp_count
        - seq_index * row_share
        + jnp.arange(per_peer, dtype=jnp.int32)[None, :]
    ).reshape(-1)
    placer = (target[None, :] == jnp.arange(row_share, dtype=jnp.int32)[:, None]).astype(
        jnp.bfloat16
    )
    own_rows = jnp.dot(
        placer, incoming.reshape(tp_count * per_peer, MW), preferred_element_type=jnp.float32
    ).astype(jnp.bfloat16)
    weight_rows = image_weight
    hidden = merger_hidden(
        lax.all_gather(own_rows, "tp", axis=0, tiled=True), merge_up, merge_up_bias, weight_rows
    )
    partial_sum = jnp.dot(hidden, merge_down, preferred_element_type=jnp.float32)
    text_rows = (
        text_embeds.reshape(row_share, tp_count, column_count)
        .transpose(1, 0, 2)
        .reshape(TOK_SEQ, column_count)
        .astype(jnp.float32)
    )
    text_rows = text_rows * (1.0 - image_weight)[:, None]
    column_start = tensor_parallel_index * column_count
    single_key_head = tensor_parallel_index * local_heads // (LOCAL_QUERY_HEAD // KEY_VALUE_HEADS)
    key_weight = lax.dynamic_slice_in_dim(
        key_value_weight, single_key_head * HEAD_DIMENSION, HEAD_DIMENSION, 1
    )
    value_matrix = lax.dynamic_slice_in_dim(
        key_value_weight,
        KEY_VALUE_HEADS * HEAD_DIMENSION + single_key_head * HEAD_DIMENSION,
        HEAD_DIMENSION,
        1,
    )
    key_bias = lax.dynamic_slice_in_dim(
        key_value_bias, single_key_head * HEAD_DIMENSION, HEAD_DIMENSION
    )
    bias_of_value = lax.dynamic_slice_in_dim(
        key_value_bias,
        KEY_VALUE_HEADS * HEAD_DIMENSION + single_key_head * HEAD_DIMENSION,
        HEAD_DIMENSION,
    )
    current = lax.dynamic_slice_in_dim(partial_sum, column_start, column_count, 1)
    term = lax.dynamic_update_slice_in_dim(partial_sum, current + text_rows, column_start, 1)
    summed = lax.psum(term, "tp")
    residual = summed + image_weight[:, None] * merge_down_bias[None, :]
    scale_rows = lax.rsqrt(jnp.mean(residual * residual, axis=1) + EPS)
    normed_rows = (residual * scale_rows[:, None] * attn_gain[None, :]).astype(jnp.bfloat16)
    query = jnp.dot(normed_rows, q_weight, preferred_element_type=jnp.float32)
    key_tensor = jnp.dot(normed_rows, key_weight, preferred_element_type=jnp.float32)
    value_tensor = jnp.dot(normed_rows, value_matrix, preferred_element_type=jnp.float32)
    residual_columns = lax.dynamic_slice_in_dim(residual, column_start, column_count, 1)
    query = apply_rotation(
        (query + q_bias).reshape(TOK_SEQ, local_heads, HEAD_DIMENSION), cosine_values, sine_lookup
    ).astype(jnp.bfloat16)
    key_tensor = (
        apply_rotation(
            (key_tensor + key_bias).reshape(TOK_SEQ, 1, HEAD_DIMENSION), cosine_values, sine_lookup
        )
        .reshape(TOK_SEQ, HEAD_DIMENSION)
        .astype(jnp.bfloat16)
    )
    value_tensor = (value_tensor + bias_of_value).astype(jnp.bfloat16)
    score_scale = HEAD_DIMENSION ** (-0.5)
    best_score = jnp.full((local_heads, TOK_SEQ), -1e30, jnp.float32)
    key_piece, value_piece = sent_together((key_tensor, value_tensor), "seq", 0, 1)
    global_row = jnp.arange(key_piece.shape[0], dtype=jnp.int32)
    inner_row = global_row % TOK_SEQ
    key_position = (
        global_row // TOK_SEQ * TOK_SEQ + inner_row % row_share * tp_count + inner_row // row_share
    )
    scores = (
        jnp.einsum("qhd,kd->hqk", query, key_piece, preferred_element_type=jnp.float32)
        * score_scale
    )
    allowed = key_position[None, None, :] <= positions[None, :, None]
    scores = jnp.where(allowed, scores, -1e30)
    fresh_best = jnp.maximum(best_score, jnp.max(scores, axis=2))
    weights = jnp.where(allowed, jnp.exp(scores - fresh_best[:, :, None]), 0.0)
    total_weight = jnp.sum(weights, axis=2)
    accumulated = jnp.einsum(
        "hqk,kd->hqd", weights.astype(jnp.bfloat16), value_piece, preferred_element_type=jnp.float32
    )
    best_score, total_weight, accumulated = (fresh_best, total_weight, accumulated)
    attention = (
        (accumulated / total_weight[:, :, None])
        .astype(jnp.bfloat16)
        .transpose(1, 0, 2)
        .reshape(TOK_SEQ, local_heads * HEAD_DIMENSION)
    )
    weight_cols = lax.all_to_all(o_weight, "tp", split_axis=1, concat_axis=0, tiled=True)
    weight_rows = weight_cols
    mixed = jnp.dot(
        gathered_copies(attention, "tp", 1), weight_rows, preferred_element_type=jnp.float32
    )
    output_rows = residual_columns + mixed
    return (
        output_rows.reshape(tp_count, row_share, column_count)
        .transpose(1, 0, 2)
        .reshape(TOK_SEQ, column_count)
        .astype(jnp.bfloat16)
    )


def solution(mesh):
    return jax.shard_map(
        per_device,
        mesh=mesh,
        in_specs=(
            P(("seq", "tp"), None),
            P(),
            P(),
            P(),
            P(None, "tp"),
            P("tp"),
            P("tp", None),
            P(),
            P("seq", "tp"),
            P(),
            P(None, "tp"),
            P("tp"),
            P(),
            P(),
            P("tp", None),
        ),
        out_specs=P("seq", "tp"),
        check_vma=False,
    )
```

profile of v0, /device:TPU:0, one launch (start us, length us, event | category | flops | bytes accessed | tf_op | source)
XLA Modules:
  0.0 355.0 jit_solution(4391008567551796274)
XLA Ops:
  11.2 1.3 convert_reduce_fusion
  12.5 1.4 fusion.10
  13.9 2.3 fusion.13
  16.2 2.3 reshape.441
  19.1 2.4 convolution_convert_fusion
  21.5 2.3 reshape.442
  23.8 7.2 %all-to-all-start = ((bf16[16,5,5120]{2,1,0:T(8,128)(2,1)}), bf16[16,5,5120]{2,1,0:T(8,128)(2,1)}, u32[]{:S(2)}, u32[]{:S(2)}) async-start(bf16[16,5,5120]{2,1,0:T(8,128)(2,1)} %reshape.442), calls=%async_computation | async-start | bytes 2621440 | tf_op jit(solution)/shard_map/all_to_all | solution.py:153
  31.2 20.6 %all-to-all-done = bf16[16,5,5120]{2,1,0:T(8,128)(2,1)} async-done(((bf16[16,5,5120]{2,1,0:T(8,128)(2,1)}), bf16[16,5,5120]{2,1,0:T(8,128)(2,1)}, u32[]{:S(2)}, u32[]{:S(2)}) %all-to-all-start) | async-done | bytes 819232 | tf_op jit(solution)/shard_map/all_to_all | solution.py:153
  51.9 2.2 reshape.443
  54.1 2.1 convolution_convert_fusion.1
  56.2 1.1 copy.26
  57.4 1.1 copy.27
  59.1 52.2 %all-gather.3.cloned.1.call-done = bf16[512,5120]{1,0:T(8,128)(2,1)} async-done(((bf16[32,5120]{1,0:T(8,128)(2,1)}), bf16[512,5120]{1,0:T(8,128)(2,1)}) %all-gather.3.cloned.1.call-update) | async-done | bytes 5242896 | tf_op jit(solution)/shard_map/all_gather | solution.py:167
  111.3 11.4 %fusion.47 = f32[512,3584]{1,0:T(8,128)} fusion(bf16[320,3584]{1,0:T(8,128)(2,1)} %param.21, bf16[512,5120]{1,0:T(8,128)(2,1)} %all-gather.3.cloned.1.call-done, bf16[5120,320]{0,1:T(8,128)(2,1)S(1)} %copy-done, f32[512]{0:T(512)S(1)} %get-tuple-element.28, f32[320]{0:T(512)S(1)} %copy-done.10), kind=kOutput, calls=%fused_computation.58 | convolution fusion | flops 2863104000 | bytes 18156800 | tf_op jit(solution)/shard_map/dot_general | solution.py:169
  122.7 1.6 fusion.48
  124.3 3.5 dynamic_update_slice.3
  129.1 130.4 %all-reduce.2.cloned.1.call-done = f32[512,3584]{1,0:T(8,128)} async-done(((f32[512,3584]{1,0:T(8,128)}), f32[512,3584]{1,0:T(8,128)}) %all-reduce.2.cloned.1.call-update) | async-done | bytes 7340048 | tf_op jit(solution)/shard_map/psum | solution.py:198
  259.5 4.2 %multiply_reduce_fusion = (f32[512]{0:T(512)S(1)}, f32[512,3584]{1,0:T(8,128)S(1)}) fusion(f32[512,3584]{1,0:T(8,128)} %all-reduce.2.cloned.1.call-done, f32[3584]{0:T(1024)S(1)} %copy-done.6, f32[512]{0:T(512)S(1)} %get-tuple-element.28), kind=kLoop, calls=%fused_computation.3 | loop fusion | flops 7339520 | bytes 14698496 | tf_op jit(solution)/shard_map/reduce_sum | solution.py:200
  263.8 1.1 multiply_convert_fusion
  264.8 1.8 copy-done.3
  266.7 3.2 convolution_add_fusion.3
  270.0 2.6 fusion.23
  272.6 1.0 fusion.88
  274.4 1.3 copy.28
  275.7 5.4 %all-to-all-start.2 = ((bf16[128,16,224]{0,2,1:T(8,128)(2,1)}), bf16[128,16,224]{0,2,1:T(8,128)(2,1)}, u32[]{:S(2)}, u32[]{:S(2)}) async-start(bf16[128,16,224]{0,2,1:T(8,128)(2,1)} %bitcast.18), calls=%async_computation.2 | async-start | bytes 1835008 | tf_op jit(solution)/shard_map/all_to_all | solution.py:244
  281.2 3.4 convolution_add_fusion.1
  284.6 15.3 %all-gather.5.cloned.1.call-done = bf16[4096,256]{0,1:T(8,128)(2,1)} async-done(((bf16[512,256]{0,1:T(8,128)(2,1)}), bf16[4096,256]{0,1:T(8,128)(2,1)}) %all-gather.5.cloned.1.call-update) | async-done | bytes 2097168 | tf_op jit(solution)/shard_map/all_gather | solution.py:18
  299.9 3.8 %fusion = (f32[512]{0:T(512)S(1)}, f32[4096,512]{1,0:T(8,128)S(1)}) fusion(s32[512]{0:T(512)S(1)} %fusion.123, s32[4096]{0:T(1024)S(1)} %fusion.106, f32[512,64]{0,1:T(8,128)S(1)} %convert_multiply_fusion, f32[512,128]{0,1:T(8,128)S(1)} %convolution_add_fusion.1, f32[512,64]{0,1:T(8,128)S(1)} %get-tuple-element.16, f32[512,64]{0,1:T(8,128)S(1)} %get-tuple-element.15, ...), kind=kOutput, calls=%fused_computation.5 | convolution fusion | flops 545652224 | bytes 10113024 | tf_op jit(solution)/shard_map/qhd,kd->hqk/dot_general | solution.py:226
  303.7 2.9 fusion.1
  306.6 3.0 fusion.27
  310.0 35.3 %all_to_all.26 = bf16[16,512,128]{2,1,0:T(8,128)(2,1)S(1)} all-to-all(bf16[16,512,128]{2,1,0:T(8,128)(2,1)S(1)} %broadcast_in_dim.60), channel_id=1, replica_groups=mesh['seq'=8,'tp'=16] {'tp'}, dimensions={0} | all-to-all | bytes 4194304 | tf_op jit(solution)/shard_map/all_to_all | solution.py:27
  345.4 2.1 fusion.20
  (65 shorter events, 7.6 us)
Async XLA Ops:
  6.5 104.8 %copy-start = (bf16[5120,320]{0,1:T(8,128)(2,1)S(1)}, bf16[5120,320]{0,1:T(8,128)(2,1)}, u32[]{:S(2)}) copy-start(bf16[5120,320]{0,1:T(8,128)(2,1)} %param.19) | copy-start | bytes 9830404
  21.5 89.8 %copy-start.10 = (f32[320]{0:T(512)S(1)}, f32[320]{0:T(512)}, u32[]{:S(2)}) copy-start(f32[320]{0:T(512)} %param.20) | copy-start | bytes 3844
  23.8 28.1 %all-to-all-start = ((bf16[16,5,5120]{2,1,0:T(8,128)(2,1)}), bf16[16,5,5120]{2,1,0:T(8,128)(2,1)}, u32[]{:S(2)}, u32[]{:S(2)}) async-start(bf16[16,5,5120]{2,1,0:T(8,128)(2,1)} %reshape.442), calls=%async_computation | async-start | bytes 2621440 | tf_op jit(solution)/shard_map/all_to_all | solution.py:153
  31.0 80.3 %all-gather.3.cloned.1.call-start = ((), (), s32[]{:S(2)}) async-start(), calls=%async_computation.3 | async-start | bytes 5570560 | tf_op jit(solution)/shard_map/all_gather | solution.py:167
  56.2 203.3 %all-reduce.2.cloned.1.call-start = ((), (), s32[]{:S(2)}) async-start(), calls=%async_computation.4 | async-start | bytes 14680064 | tf_op jit(solution)/shard_map/psum | solution.py:198
  122.7 136.8 %copy-start.6 = (f32[3584]{0:T(1024)S(1)}, f32[3584]{0:T(1024)}, u32[]{:S(2)}) copy-start(f32[3584]{0:T(1024)} %param.22) | copy-start | bytes 43012
  127.8 172.1 %all-gather.5.cloned.1.call-start = ((), (), s32[]{:S(2)}) async-start(), calls=%async_computation.5 | async-start | bytes 2359296 | tf_op jit(solution)/shard_map/all_gather | solution.py:18
  129.0 134.7 %copy-start.7 = (f32[3584]{0:T(1024)S(1)}, f32[3584]{0:T(1024)}, u32[]{:S(2)}) copy-start(f32[3584]{0:T(1024)} %param.24) | copy-start | bytes 43012
  263.7 3.0 copy-start.3
  266.7 5.9 %copy-start.2 = (bf16[512,3584]{1,0:T(8,128)(2,1)}, bf16[512,3584]{1,0:T(8,128)(2,1)S(1)}, u32[]{:S(2)}) copy-start(bf16[512,3584]{1,0:T(8,128)(2,1)S(1)} %multiply_convert_fusion) | copy-start | bytes 11010052
  269.9 4.5 %copy-start.4 = (bf16[128,3584]{1,0:T(8,128)(2,1)S(1)}, bf16[128,3584]{1,0:T(8,128)(2,1)}, u32[]{:S(2)}) copy-start(bf16[128,3584]{1,0:T(8,128)(2,1)} %param.29) | copy-start | bytes 2752516
  269.9 11.2 %copy-start.5 = (bf16[3584,128]{1,0:T(8,128)(2,1)S(1)}, bf16[3584,128]{1,0:T(8,128)(2,1)}, u32[]{:S(2)}) copy-start(bf16[3584,128]{1,0:T(8,128)(2,1)} %param.25) | copy-start | bytes 2752516
  270.0 11.2 %copy-start.8 = (f32[128]{0:T(128)S(1)}, f32[128]{0:T(128)}, u32[]{:S(2)}) copy-start(f32[128]{0:T(128)} %param.26) | copy-start | bytes 1540
  275.7 33.9 %all-to-all-start.2 = ((bf16[128,16,224]{0,2,1:T(8,128)(2,1)}), bf16[128,16,224]{0,2,1:T(8,128)(2,1)}, u32[]{:S(2)}, u32[]{:S(2)}) async-start(bf16[128,16,224]{0,2,1:T(8,128)(2,1)} %bitcast.18), calls=%async_computation.2 | async-start | bytes 1835008 | tf_op jit(solution)/shard_map/all_to_all | solution.py:244
  303.7 2.9 copy-start.9
  306.6 41.9 %copy-start.1 = (bf16[5120,320]{0,1:T(8,128)(2,1)S(1)}, bf16[5120,320]{0,1:T(8,128)(2,1)}, u32[]{:S(2)}) copy-start(bf16[5120,320]{0,1:T(8,128)(2,1)} %param.19) | copy-start | bytes 9830404
Sparse Core Ops, SparseCore 0:
  56.3 54.9 all-gather.2
  127.9 131.4 all-reduce.1
  274.5 25.3 all-gather.4
where the time goes:
time: 356 us; the launch traced here: 355 us
  waiting for transfers between devices  219 us (62%)
  blocking collectives  35.3 us (10%)
  matrix products  34.1 us (10%)
  local copies, waits for them, and re-layouts  20.4 us (6%)
  other arithmetic  18.2 us (5%)
  between operations  15.5 us (4%)
  starting transfers between devices  12.9 us (4%)
    psum x1, waiting for transfers between devices, per_device(): summed = lax.psum(term, 'tp')  130 us
    all_gather x1, waiting for transfers between devices, per_device(): lax.all_gather(own_rows, 'tp', axis=0, tiled=True)  52.2 us
    all_to_all x1, blocking collectives, copy_for_each(): lax.all_to_all(jnp.broadcast_to(shard[None], (peers, *shard.shape)), axis...  35.3 us
    all_to_all x1, waiting for transfers between devices, per_device(): lax.all_to_all(outgoing, 'tp', split_axis=0, concat_axis=0, tiled=True)  20.6 us
    all_gather x1, waiting for transfers between devices, sent_together(): out, at, done = (lax.all_gather(both, axis, axis=dim, tiled=True), 0, [])  15.3 us
    dot_general x1, matrix products, per_device(): jnp.dot(hidden, merge_down, preferred_element_type=jnp.float32)  11.4 us
    all_to_all x1, starting transfers between devices, per_device(): lax.all_to_all(outgoing, 'tp', split_axis=0, concat_axis=0, tiled=True)  7.19 us
  transfers between devices with their start and end apart: 5, of which 4 were waited for; matrix products, arithmetic and copies ran while one was open for 5% of the time, Pallas kernels for 0%

commit v1 on v0

--- a/solution.py
+++ b/solution.py
@@ -195,7 +195,9 @@
     )
     current = lax.dynamic_slice_in_dim(partial_sum, column_start, column_count, 1)
     term = lax.dynamic_update_slice_in_dim(partial_sum, current + text_rows, column_start, 1)
-    summed = lax.psum(term, "tp")
+    summed = term
+    for hop in (1, 2, 4, 8):
+        summed = summed + lax.ppermute(summed, "tp", [(dev, dev ^ hop) for dev in range(16)])
     residual = summed + image_weight[:, None] * merge_down_bias[None, :]
     scale_rows = lax.rsqrt(jnp.mean(residual * residual, axis=1) + EPS)
     normed_rows = (residual * scale_rows[:, None] * attn_gain[None, :]).astype(jnp.bfloat16)

time: 356 us -> 884 us (2.48)
  waiting for transfers between devices: 219 us -> 715 us
  other arithmetic: 18.2 us -> 41.9 us
  starting transfers between devices: 12.9 us -> 22.4 us
    ppermute x0 -> x4, waiting for transfers between devices: none -> 627 us  [per_device(): lax.ppermute(summed, 'tp', [(dev, dev ^ hop) for dev in range(16)])]
    psum x1 -> x0, waiting for transfers between devices: 130 us -> none  [per_device(): summed = lax.psum(term, 'tp')]
    add x0 -> x3, other arithmetic: none -> 21.3 us  [per_device(): summed + lax.ppermute(summed, 'tp', [(dev, dev ^ hop) for dev in range(16)])]
    ppermute x0 -> x4, starting transfers between devices: none -> 9.64 us  [per_device(): lax.ppermute(summed, 'tp', [(dev, dev ^ hop) for dev in range(16)])]
  transfers between devices with their start and end apart: 5 -> 8, of which waited for: 4 -> 7; matrix products, arithmetic and copies ran while one was open for 5% -> 2% of each run, Pallas kernels for 0% -> 0%
where the time goes in v1:
time: 884 us; the launch traced here: 883 us
  waiting for transfers between devices  715 us (81%)
  other arithmetic  41.9 us (5%)
  blocking collectives  35.3 us (4%)
  matrix products  34.1 us (4%)
  starting transfers between devices  22.4 us (3%)
  local copies, waits for them, and re-layouts  18.5 us (2%)
  between operations  15.8 us (2%)
    ppermute x4, waiting for transfers between devices, per_device(): lax.ppermute(summed, 'tp', [(dev, dev ^ hop) for dev in range(16)])  627 us
    all_gather x1, waiting for transfers between devices, per_device(): lax.all_gather(own_rows, 'tp', axis=0, tiled=True)  52.2 us
    all_to_all x1, blocking collectives, copy_for_each(): lax.all_to_all(jnp.broadcast_to(shard[None], (peers, *shard.shape)), axis...  35.3 us
    add x3, other arithmetic, per_device(): summed + lax.ppermute(summed, 'tp', [(dev, dev ^ hop) for dev in range(16)])  21.3 us
    all_to_all x1, waiting for transfers between devices, per_device(): lax.all_to_all(outgoing, 'tp', split_axis=0, concat_axis=0, tiled=True)  20.6 us
  transfers between devices with their start and end apart: 8, of which 7 were waited for; matrix products, arithmetic and copies ran while one was open for 2% of the time, Pallas kernels for 0%

profile of v1, /device:TPU:0, one launch (start us, length us, event | category | flops | bytes accessed | tf_op | source)
XLA Modules:
  0.0 883.0 jit_solution(17499374993265170354)
XLA Ops:
  13.9 2.3 fusion.13
  16.2 2.3 reshape.441
  19.1 2.4 convolution_convert_fusion
  21.5 2.2 reshape.442
  23.8 7.2 all-to-all-start
  31.2 20.6 %all-to-all-done = bf16[16,5,5120]{2,1,0:T(8,128)(2,1)} async-done(((bf16[16,5,5120]{2,1,0:T(8,128)(2,1)}), bf16[16,5,5120]{2,1,0:T(8,128)(2,1)}, u32[]{:S(2)}, u32[]{:S(2)}) %all-to-all-start) | async-done | bytes 819232 | tf_op jit(solution)/shard_map/all_to_all | solution.py:153
  51.8 2.2 reshape.443
  54.0 2.1 convolution_convert_fusion.1
  59.0 52.2 %all-gather.3.cloned.1.call-done = bf16[512,5120]{1,0:T(8,128)(2,1)} async-done(((bf16[32,5120]{1,0:T(8,128)(2,1)}), bf16[512,5120]{1,0:T(8,128)(2,1)}) %all-gather.3.cloned.1.call-update) | async-done | bytes 5242896 | tf_op jit(solution)/shard_map/all_gather | solution.py:167
  111.3 11.4 %fusion.41 = f32[512,3584]{1,0:T(8,128)} fusion(bf16[320,3584]{1,0:T(8,128)(2,1)} %param.21, bf16[512,5120]{1,0:T(8,128)(2,1)} %all-gather.3.cloned.1.call-done, bf16[5120,320]{0,1:T(8,128)(2,1)S(1)} %copy-done, f32[512]{0:T(512)S(1)} %get-tuple-element.28, f32[320]{0:T(512)S(1)} %copy-done.10), kind=kOutput, calls=%fused_computation.56 | convolution fusion | flops 2863104000 | bytes 18156800 | tf_op jit(solution)/shard_map/dot_general | solution.py:169
  124.2 3.5 dynamic_update_slice.3
  127.7 1.8 collective-permute-start
  129.5 158.1 %collective-permute-done = f32[512,3584]{1,0:T(8,128)} collective-permute-done((f32[512,3584]{1,0:T(8,128)}, f32[512,3584]{1,0:T(8,128)}, u32[]{:S(2)}, u32[]{:S(2)}) %collective-permute-start) | collective-permute-done | bytes 7340064 | tf_op jit(solution)/shard_map/ppermute | solution.py:200
  287.6 6.5 add.374
  294.1 3.5 collective-permute-start.1
  297.6 157.1 %collective-permute-done.1 = f32[512,3584]{1,0:T(8,128)} collective-permute-done((f32[512,3584]{1,0:T(8,128)S(1)}, f32[512,3584]{1,0:T(8,128)}, u32[]{:S(2)}, u32[]{:S(2)}) %collective-permute-start.1) | collective-permute-done | bytes 7340064 | tf_op jit(solution)/shard_map/ppermute | solution.py:200
  454.7 7.4 add.375
  463.5 156.7 %collective-permute-done.2 = f32[512,3584]{1,0:T(8,128)S(1)} collective-permute-done((f32[512,3584]{1,0:T(8,128)}, f32[512,3584]{1,0:T(8,128)S(1)}, u32[]{:S(2)}, u32[]{:S(2)}) %collective-permute-start.2) | collective-permute-done | bytes 7340064 | tf_op jit(solution)/shard_map/ppermute | solution.py:200
  620.2 7.4 add.376
  627.6 2.9 collective-permute-start.3
  631.5 155.0 %collective-permute-done.3 = f32[512,3584]{1,0:T(8,128)} collective-permute-done((f32[512,3584]{1,0:T(8,128)}, f32[512,3584]{1,0:T(8,128)}, u32[]{:S(2)}, u32[]{:S(2)}) %collective-permute-start.3) | collective-permute-done | bytes 7340064 | tf_op jit(solution)/shard_map/ppermute | solution.py:200
  786.5 6.5 multiply_reduce_fusion
  794.3 3.3 convolution_add_fusion.3
  797.7 2.6 fusion.17
  803.3 5.5 all-to-all-start.2
  808.9 3.4 convolution_add_fusion.1
  812.3 15.3 %all-gather.5.cloned.1.call-done = bf16[4096,256]{0,1:T(8,128)(2,1)} async-done(((bf16[512,256]{0,1:T(8,128)(2,1)}), bf16[4096,256]{0,1:T(8,128)(2,1)}) %all-gather.5.cloned.1.call-update) | async-done | bytes 2097168 | tf_op jit(solution)/shard_map/all_gather | solution.py:18
  827.6 3.8 fusion
  831.4 2.9 fusion.1
  834.3 3.0 fusion.21
  837.7 35.3 %all_to_all.26 = bf16[16,512,128]{2,1,0:T(8,128)(2,1)S(1)} all-to-all(bf16[16,512,128]{2,1,0:T(8,128)(2,1)S(1)} %broadcast_in_dim.60), channel_id=1, replica_groups=mesh['seq'=8,'tp'=16] {'tp'}, dimensions={0} | all-to-all | bytes 4194304 | tf_op jit(solution)/shard_map/all_to_all | solution.py:27
  873.0 2.1 add_convert_fusion
  (73 shorter events, 18.7 us)
Async XLA Ops:
  6.5 104.7 %copy-start = (bf16[5120,320]{0,1:T(8,128)(2,1)S(1)}, bf16[5120,320]{0,1:T(8,128)(2,1)}, u32[]{:S(2)}) copy-start(bf16[5120,320]{0,1:T(8,128)(2,1)} %param.19) | copy-start | bytes 9830404
  13.9 97.4 %copy-start.10 = (f32[320]{0:T(512)S(1)}, f32[320]{0:T(512)}, u32[]{:S(2)}) copy-start(f32[320]{0:T(512)} %param.20) | copy-start | bytes 3844
  23.8 28.1 %all-to-all-start = ((bf16[16,5,5120]{2,1,0:T(8,128)(2,1)}), bf16[16,5,5120]{2,1,0:T(8,128)(2,1)}, u32[]{:S(2)}, u32[]{:S(2)}) async-start(bf16[16,5,5120]{2,1,0:T(8,128)(2,1)} %reshape.442), calls=%async_computation | async-start | bytes 2621440 | tf_op jit(solution)/shard_map/all_to_all | solution.py:153
  31.0 80.3 %all-gather.3.cloned.1.call-start = ((), (), s32[]{:S(2)}) async-start(), calls=%async_computation.3 | async-start | bytes 5570560 | tf_op jit(solution)/shard_map/all_gather | solution.py:167
  56.1 771.4 %all-gather.5.cloned.1.call-start = ((), (), s32[]{:S(2)}) async-start(), calls=%async_computation.4 | async-start | bytes 2359296 | tf_op jit(solution)/shard_map/all_gather | solution.py:18
  127.7 159.9 %collective-permute-start = (f32[512,3584]{1,0:T(8,128)}, f32[512,3584]{1,0:T(8,128)}, u32[]{:S(2)}, u32[]{:S(2)}) collective-permute-start(f32[512,3584]{1,0:T(8,128)} %dynamic_update_slice.3), channel_id=1, source_target_pairs={{0,1},{1,0},{2,3},{3,2},{4,5},{5,4},{6,7},{7,6},{8,9},{9,8},{10,11... | collective-permute-start | bytes 22020104 | tf_op jit(solution)/shard_map/ppermute | solution.py:200
  294.1 160.6 %collective-permute-start.1 = (f32[512,3584]{1,0:T(8,128)S(1)}, f32[512,3584]{1,0:T(8,128)}, u32[]{:S(2)}, u32[]{:S(2)}) collective-permute-start(f32[512,3584]{1,0:T(8,128)S(1)} %add.374), channel_id=1, source_target_pairs={{0,2},{1,3},{2,0},{3,1},{4,6},{5,7},{6,4},{7,5},{8,10},{9,11},{10,... | collective-permute-start | bytes 22020104 | tf_op jit(solution)/shard_map/ppermute | solution.py:200
  462.1 324.4 %copy-start.7 = (f32[3584]{0:T(1024)S(1)}, f32[3584]{0:T(1024)}, u32[]{:S(2)}) copy-start(f32[3584]{0:T(1024)} %param.22) | copy-start | bytes 43012
  462.1 158.1 %collective-permute-start.2 = (f32[512,3584]{1,0:T(8,128)}, f32[512,3584]{1,0:T(8,128)S(1)}, u32[]{:S(2)}, u32[]{:S(2)}) collective-permute-start(f32[512,3584]{1,0:T(8,128)} %add.375), channel_id=1, source_target_pairs={{0,4},{1,5},{2,6},{3,7},{4,0},{5,1},{6,2},{7,3},{8,12},{9,13},{10,... | collective-permute-start | bytes 22020104 | tf_op jit(solution)/shard_map/ppermute | solution.py:200
  627.6 158.8 %collective-permute-start.3 = (f32[512,3584]{1,0:T(8,128)}, f32[512,3584]{1,0:T(8,128)}, u32[]{:S(2)}, u32[]{:S(2)}) collective-permute-start(f32[512,3584]{1,0:T(8,128)} %add.376), channel_id=1, source_target_pairs={{0,8},{1,9},{2,10},{3,11},{4,12},{5,13},{6,14},{7,15},{8,0},{9,1},... | collective-permute-start | bytes 22020104 | tf_op jit(solution)/shard_map/ppermute | solution.py:200
  631.5 161.5 %copy-start.6 = (f32[3584]{0:T(1024)S(1)}, f32[3584]{0:T(1024)}, u32[]{:S(2)}) copy-start(f32[3584]{0:T(1024)} %param.24) | copy-start | bytes 43012
  793.0 4.6 copy-start.3
  794.2 7.0 copy-start.2
  794.3 7.8 copy-start.4
  797.6 11.2 %copy-start.5 = (bf16[3584,128]{1,0:T(8,128)(2,1)S(1)}, bf16[3584,128]{1,0:T(8,128)(2,1)}, u32[]{:S(2)}) copy-start(bf16[3584,128]{1,0:T(8,128)(2,1)} %param.25) | copy-start | bytes 2752516
  797.6 11.2 %copy-start.8 = (f32[128]{0:T(128)S(1)}, f32[128]{0:T(128)}, u32[]{:S(2)}) copy-start(f32[128]{0:T(128)} %param.26) | copy-start | bytes 1540
  803.3 33.9 %all-to-all-start.2 = ((bf16[128,16,224]{0,2,1:T(8,128)(2,1)}), bf16[128,16,224]{0,2,1:T(8,128)(2,1)}, u32[]{:S(2)}, u32[]{:S(2)}) async-start(bf16[128,16,224]{0,2,1:T(8,128)(2,1)} %bitcast.18), calls=%async_computation.2 | async-start | bytes 1835008 | tf_op jit(solution)/shard_map/all_to_all | solution.py:246
  831.4 2.9 copy-start.9
  834.3 41.9 %copy-start.1 = (bf16[5120,320]{0,1:T(8,128)(2,1)S(1)}, bf16[5120,320]{0,1:T(8,128)(2,1)}, u32[]{:S(2)}) copy-start(bf16[5120,320]{0,1:T(8,128)(2,1)} %param.19) | copy-start | bytes 9830404
Sparse Core Ops, SparseCore 0:
  56.3 54.9 all-gather.2
  802.1 25.3 all-gather.4
